TPU v7x, 512 devices: a whole 4x8x8 slice. The times are simulated.
512 devices in a mesh: node: 32 (over z, x_lo, core), local: 16 (over x_hi, y).
Axes of the slice: x: 4 (x_hi: 2, x_lo: 2; x = x_hi * 2 + x_lo), y: 8, z: 8, core: 2. Of those that a mesh axis runs over, the one named last changes fastest.
Arguments:
- tokens: bfloat16 [2048, 4096], P('local', 'node'), may hold values from -6 to 6
- gate_up_codes: bfloat16 [2, 4096, 14336], P(None, 'local', 'node'), may hold values from -127 to 127
- gate_up_scales: bfloat16 [2, 32, 14336], P(None, 'local', 'node'), may hold values from 2.9921532e-05 to 0.00029945374
- d_hidden: bfloat16 [2048, 14336], P('local', 'node'), may hold values from -6 to 6
Outputs:
- hidden: bfloat16 [2048, 14336], P('local', 'node')
- d_tokens: bfloat16 [2048, 4096], P('local', 'node')
- grad_gate_up: float32 [2, 4096, 14336], P(None, 'local', 'node')
All inputs are finite; a program needn't handle non-finite values.
Results may differ from a plain program's by a relative error of at most 0.023.
Values may be sent and summed in bfloat16 or wider, within the bound.
A program may use at most 128 MiB of HBM per device.

v0:
```python
import math
import jax
import jax.numpy as jnp
from jax import lax
from jax.sharding import PartitionSpec as P

BLOCK = 128


def from_everyone(array, axis):
    length = lax.axis_size(axis)
    return lax.all_to_all(
        jnp.broadcast_to(array[None], (length, *array.shape)), axis, 0, 0, tiled=True
    )


def in_order(pieces, dim):
    pieces = jnp.moveaxis(pieces, 0, dim)
    lengths = pieces.shape
    return pieces.reshape(*lengths[:dim], lengths[dim] * lengths[dim + 1], *lengths[dim + 2 :])


def gather_directly(array, axis, dim):
    pieces = from_everyone(array, axis)
    return in_order(pieces, dim)


def cut_along(array, dim, length):
    before, after = (array.shape[:dim], array.shape[dim + 1 :])
    return jnp.moveaxis(array.reshape(*before, length, -1, *after), dim, 0)


def sent_and_summed(array, axis, dim):
    pieces = cut_along(array, dim, lax.axis_size(axis))
    arrived = lax.all_to_all(pieces, axis, split_axis=0, concat_axis=0, tiled=True)
    return arrived.astype(jnp.float32).sum(axis=0)


def sent_together(arrays, axis, dim, along):
    both = jnp.concatenate(arrays, axis=along)
    out, at, outs = (lax.all_gather(both, axis, axis=dim, tiled=True), 0, [])
    for a in arrays:
        outs.append(lax.slice_in_dim(out, at, at + a.shape[along], axis=along))
        at += a.shape[along]
    return tuple(outs)


def dequant(codes, scales):
    shape = codes.shape
    blocked = codes.astype(jnp.float32).reshape(shape[:-2] + (shape[-2] // BLOCK, BLOCK, shape[-1]))
    weight = blocked * scales.astype(jnp.float32)[..., :, None, :]
    return weight.reshape(shape).astype(jnp.bfloat16)


def body(tokens, gate_up_codes, gate_up_scales, d_hidden):
    rows = tokens.shape[0]
    local_count = lax.axis_size("local")
    features = gather_directly(tokens, "node", 1)
    width = features.shape[1]
    all_codes, all_scales = (
        lax.all_gather(gate_up_codes, "local", axis=1, tiled=True),
        lax.all_gather(gate_up_scales, "local", axis=1, tiled=True),
    )
    w_gu = dequant(all_codes, all_scales)
    group = w_gu.shape[2]
    gate = jnp.dot(features, w_gu[0], preferred_element_type=jnp.float32)
    up = jnp.dot(features, w_gu[1], preferred_element_type=jnp.float32)
    sigmoid_gate = jax.nn.sigmoid(gate)
    active = gate * sigmoid_gate
    hidden = (active * up).astype(jnp.bfloat16)
    grad_in = d_hidden.astype(jnp.float32)
    d_gate = (grad_in * up * sigmoid_gate * (1.0 + gate * (1.0 - sigmoid_gate))).astype(
        jnp.bfloat16
    )
    d_up = (grad_in * active).astype(jnp.bfloat16)
    term = lax.dot_general(
        d_gate, w_gu[0], (((1,), (1,)), ((), ())), preferred_element_type=jnp.float32
    )
    term = term + lax.dot_general(
        d_up, w_gu[1], (((1,), (1,)), ((), ())), preferred_element_type=jnp.float32
    )
    rounded = lax.optimization_barrier(term.astype(jnp.bfloat16)).astype(jnp.float32)
    d_tokens = sent_and_summed(rounded.astype(jnp.bfloat16), "node", 1).astype(jnp.bfloat16)
    factor = 1.0 / math.sqrt(rows * local_count)
    owned = width // local_count
    columns = lax.all_to_all(features, "local", split_axis=1, concat_axis=0, tiled=True)
    gate_all, up_all = sent_together((d_gate, d_up), "local", 0, 1)
    both_all = jnp.concatenate(
        [gate_all.reshape(local_count, rows, group), up_all.reshape(local_count, rows, group)],
        axis=2,
    )
    blocks = columns.reshape(local_count, rows, owned)
    numbers = (((1,), (1,)), ((0,), (0,)))
    partial_value = lax.dot_general(
        blocks, both_all, numbers, preferred_element_type=jnp.float32
    ).astype(jnp.bfloat16)
    summed = jnp.sum(partial_value.astype(jnp.float32), axis=0) * factor
    grads = summed.reshape(owned, 2, group).transpose(1, 0, 2)
    return (hidden, d_tokens, grads)


def solution(mesh):
    placed = (
        P("local", "node"),
        P(None, "local", "node"),
        P(None, "local", "node"),
        P("local", "node"),
    )
    return jax.shard_map(
        body,
        mesh=mesh,
        in_specs=placed,
        out_specs=(P("local", "node"), P("local", "node"), P(None, "local", "node")),
        check_vma=False,
    )
```

profile of v0, /device:TPU:8, one launch (start us, length us, event | category | flops | bytes accessed | tf_op | source)
XLA Modules:
  0.0 310.7 jit_solution(12713937167241401182)
XLA Ops:
  7.2 0.0 copy-start.1
  7.2 0.0 all-gather.3.cloned.1.call-start
  7.2 0.7 all-gather.3.cloned.1.call-update
  7.9 0.9 copy.25
  8.8 1.3 broadcast_in_dim.2
  10.1 11.6 %all-to-all-start = ((bf16[32,128,128]{1,2,0:T(8,128)(2,1)}), bf16[32,128,128]{1,2,0:T(8,128)(2,1)S(1)}, u32[]{:S(2)}, u32[]{:S(2)}) async-start(bf16[32,128,128]{1,2,0:T(8,128)(2,1)} %broadcast_in_dim.2), calls=%async_computation | async-start | bytes 2097152 | tf_op jit(solution)/shard_map/all_to_all | solution.py:12
  21.7 0.0 all-gather.5.cloned.1.call-start
  21.8 0.0 copy-done.1
  21.8 38.0 %all_gather.10 = bf16[2,32,448]{2,0,1:T(2,128)(2,1)S(1)} all-gather(bf16[2,2,448]{2,0,1:T(2,128)(2,1)S(1)} %copy.22), channel_id=1, replica_groups=mesh['node'=32,'local'=16] {'local'}, dimensions={1}, use_global_device_ids=true | all-gather | bytes 60928 | tf_op jit(solution)/shard_map/all_gather | solution.py:62
  59.8 0.2 copy.24
  60.0 7.9 %mul.45 = f32[2,32,128,448]{2,1,3,0:T(8,128)} broadcast(f32[2,32,448]{1,2,0:T(8,128)S(1)} %copy.24), dimensions={0,1,3} | broadcast | bytes 14794752 | tf_op jit(solution)/shard_map/mul | solution.py:51
  67.9 16.0 %mul.46 = f32[2,4096,448]{1,2,0:T(8,128)} reshape(f32[2,32,128,448]{2,1,3,0:T(8,128)} %mul.45) | data formatting | bytes 29360128 | tf_op jit(solution)/shard_map/mul | solution.py:51
  83.8 77.0 %all-gather.3.cloned.1.call-done = bf16[2,4096,448]{1,2,0:T(8,128)(2,1)} async-done(((bf16[2,256,448]{1,2,0:T(8,128)(2,1)}), bf16[2,4096,448]{1,2,0:T(8,128)(2,1)}) %all-gather.3.cloned.1.call-update) | async-done | bytes 7340048 | tf_op jit(solution)/shard_map/all_gather | solution.py:61
  160.9 0.0 copy-start.2
  160.9 10.6 %multiply_convert_fusion = bf16[2,4096,448]{1,2,0:T(8,128)(2,1)} fusion(f32[2,4096,448]{1,2,0:T(8,128)} %mul.46, bf16[2,4096,448]{1,2,0:T(8,128)(2,1)} %all-gather.3.cloned.1.call-done), kind=kLoop, calls=%fused_computation.1 | loop fusion | flops 11010048 | bytes 29360128 | tf_op jit(solution)/shard_map/convert_element_type | solution.py:52
  171.5 0.0 all-to-all-done
  171.5 0.0 copy-start
  171.5 3.3 %fusion.8 = f32[128,448]{0,1:T(8,128)S(1)} fusion(bf16[128,4096]{0,1:T(8,128)(2,1)S(1)} %bitcast.54, bf16[2,4096,448]{1,2,0:T(8,128)(2,1)} %multiply_convert_fusion), kind=kOutput, calls=%fused_computation.17 | convolution fusion | flops 469762048 | bytes 4947968 | tf_op jit(solution)/shard_map/dot_general | solution.py:66
  174.8 0.0 copy-done.2
  174.8 0.9 copy-done
  175.7 1.8 fusion.12
  177.5 0.7 pad_maximum_fusion
  178.2 0.0 all-gather.5.cloned.1.call-update
  178.2 2.8 fusion.4
  181.0 2.8 fusion
  183.8 1.3 bitcast_bitcast_fusion
  185.1 7.8 %all-to-all-start.1 = ((bf16[32,128,128]{2,1,0:T(8,128)(2,1)}), bf16[32,128,128]{2,1,0:T(8,128)(2,1)S(1)}, u32[]{:S(2)}, u32[]{:S(2)}) async-start(bf16[32,128,128]{2,1,0:T(8,128)(2,1)} %bitcast_bitcast_fusion), calls=%async_computation.1 | async-start | bytes 2097152 | tf_op jit(solution)/shard_map/all_to_all | solution.py:35
  192.9 1.3 copy.29
  194.2 27.3 %all-to-all-done.1 = bf16[32,128,128]{2,1,0:T(8,128)(2,1)S(1)} async-done(((bf16[32,128,128]{2,1,0:T(8,128)(2,1)}), bf16[32,128,128]{2,1,0:T(8,128)(2,1)S(1)}, u32[]{:S(2)}, u32[]{:S(2)}) %all-to-all-start.1) | async-done | bytes 1048608 | tf_op jit(solution)/shard_map/all_to_all | solution.py:35
  221.5 6.0 %all-to-all-start.2 = ((bf16[128,16,256]{2,0,1:T(8,128)(2,1)}), bf16[128,16,256]{2,0,1:T(8,128)(2,1)S(1)}, u32[]{:S(2)}, u32[]{:S(2)}) async-start(bf16[128,16,256]{2,0,1:T(8,128)(2,1)} %copy.29), calls=%async_computation.2 | async-start | bytes 2097152 | tf_op jit(solution)/shard_map/all_to_all | solution.py:86
  227.5 0.8 reduce_sum.21
  228.3 66.2 %all-gather.5.cloned.1.call-done = bf16[2048,896]{0,1:T(8,128)(2,1)} async-done(((bf16[128,896]{0,1:T(8,128)(2,1)}), bf16[2048,896]{0,1:T(8,128)(2,1)}) %all-gather.5.cloned.1.call-update) | async-done | bytes 3670032 | tf_op jit(solution)/shard_map/all_gather | solution.py:41
  294.5 2.5 slice_bitcast_fusion.7
  297.0 2.2 copy_bitcast_fusion
  299.3 0.0 all-to-all-done.2
  299.3 3.6 %convert_reduce_fusion = f32[896,256]{1,0:T(8,128)S(1)} fusion(bf16[16,128,448]{1,2,0:T(8,128)(2,1)S(1)} %get-tuple-element.8, bf16[16,128,448]{1,2,0:T(8,128)(2,1)} %get-tuple-element.9, bf16[128,16,256]{2,0,1:T(8,128)(2,1)S(1)} %all-to-all-done.2), kind=kOutput, calls=%fused_computation | convolution fusion | flops 957644800 | bytes 5636096 | tf_op jit(solution)/shard_map/dot_general | solution.py:94
  302.9 1.0 broadcast_multiply_fusion
  (2 shorter events, 0.0 us)
Async XLA Ops:
  7.2 14.6 %copy-start.1 = (bf16[2,2,448]{2,1,0:T(2,128)(2,1)S(1)}, bf16[2,2,448]{2,1,0:T(2,128)(2,1)}, u32[]{:S(2)}) copy-start(bf16[2,2,448]{2,1,0:T(2,128)(2,1)} %param.6) | copy-start | bytes 10756
  7.2 153.7 %all-gather.3.cloned.1.call-start = ((), (), s32[]{:S(2)}) async-start(), calls=%async_computation.3 | async-start | bytes 7798784 | tf_op jit(solution)/shard_map/all_gather | solution.py:61
  10.1 161.5 %all-to-all-start = ((bf16[32,128,128]{1,2,0:T(8,128)(2,1)}), bf16[32,128,128]{1,2,0:T(8,128)(2,1)S(1)}, u32[]{:S(2)}, u32[]{:S(2)}) async-start(bf16[32,128,128]{1,2,0:T(8,128)(2,1)} %broadcast_in_dim.2), calls=%async_computation | async-start | bytes 2097152 | tf_op jit(solution)/shard_map/all_to_all | solution.py:12
  21.7 272.8 %all-gather.5.cloned.1.call-start = ((), (), s32[]{:S(2)}) async-start(), calls=%async_computation.4 | async-start | bytes 3899392 | tf_op jit(solution)/shard_map/all_gather | solution.py:41
  160.9 13.9 %copy-start.2 = (bf16[128,448]{0,1:T(8,128)(2,1)S(1)}, bf16[128,448]{0,1:T(8,128)(2,1)}, u32[]{:S(2)}) copy-start(bf16[128,448]{0,1:T(8,128)(2,1)} %param.7) | copy-start | bytes 344068
  171.5 4.2 %copy-start = (bf16[2,4096,448]{1,2,0:T(8,128)(2,1)S(1)}, bf16[2,4096,448]{1,2,0:T(8,128)(2,1)}, u32[]{:S(2)}) copy-start(bf16[2,4096,448]{1,2,0:T(8,128)(2,1)} %multiply_convert_fusion) | copy-start | bytes 22020100
  185.1 36.4 %all-to-all-start.1 = ((bf16[32,128,128]{2,1,0:T(8,128)(2,1)}), bf16[32,128,128]{2,1,0:T(8,128)(2,1)S(1)}, u32[]{:S(2)}, u32[]{:S(2)}) async-start(bf16[32,128,128]{2,1,0:T(8,128)(2,1)} %bitcast_bitcast_fusion), calls=%async_computation.1 | async-start | bytes 2097152 | tf_op jit(solution)/shard_map/all_to_all | solution.py:35
  221.5 77.8 %all-to-all-start.2 = ((bf16[128,16,256]{2,0,1:T(8,128)(2,1)}), bf16[128,16,256]{2,0,1:T(8,128)(2,1)S(1)}, u32[]{:S(2)}, u32[]{:S(2)}) async-start(bf16[128,16,256]{2,0,1:T(8,128)(2,1)} %copy.29), calls=%async_computation.2 | async-start | bytes 2097152 | tf_op jit(solution)/shard_map/all_to_all | solution.py:86
Sparse Core Ops, SparseCore 0:
  11.0 149.8 all-gather.2
  178.3 116.0 all-gather.4
where the time goes:
time: 312 us; the launch traced here: 311 us
  waiting for transfers between devices  171 us (55%)
  blocking collectives  38 us (12%)
  local copies, waits for them, and re-layouts  34.5 us (11%)
  starting transfers between devices  25.5 us (8%)
  matrix products  14.3 us (5%)
  between operations  14.1 us (5%)
  other arithmetic  13.1 us (4%)
    all_gather x1, waiting for transfers between devices, body(): lax.all_gather(gate_up_codes, 'local', axis=1, tiled=True)  77 us
    all_gather x1, waiting for transfers between devices, sent_together(): out, at, outs = (lax.all_gather(both, axis, axis=dim, tiled=True), 0, [])  66.2 us
    all_gather x1, blocking collectives, body(): lax.all_gather(gate_up_scales, 'local', axis=1, tiled=True)  38 us
    all_to_all x1, waiting for transfers between devices, sent_and_summed(): lax.all_to_all(pieces, axis, split_axis=0, concat_axis=0, tiled=True)  27.3 us
    mul x2, local copies, waits for them, and re-layouts, dequant(): weight = blocked * scales.astype(jnp.float32)[..., :, None, :]  23.9 us
    all_to_all x1, starting transfers between devices, from_everyone(): lax.all_to_all(jnp.broadcast_to(array[None], (length, *array.shape)), axi...  11.6 us
    convert_element_type x1, other arithmetic, dequant(): return weight.reshape(shape).astype(jnp.bfloat16)  10.6 us
    all_to_all x1, starting transfers between devices, sent_and_summed(): lax.all_to_all(pieces, axis, split_axis=0, concat_axis=0, tiled=True)  7.78 us
  transfers between devices with their start and end apart: 5, of which 3 were waited for; matrix products, arithmetic and copies ran while one was open for 16% of the time, Pallas kernels for 0%

commit v1 on v0

--- a/solution.py
+++ b/solution.py
@@ -58,7 +58,7 @@
     features = gather_directly(tokens, "node", 1)
     width = features.shape[1]
     all_codes, all_scales = (
-        lax.all_gather(gate_up_codes, "local", axis=1, tiled=True),
+        jnp.concatenate(lax.all_gather(gate_up_codes, "local"), axis=1),
         lax.all_gather(gate_up_scales, "local", axis=1, tiled=True),
     )
     w_gu = dequant(all_codes, all_scales)

time: 312 us -> 334 us (1.071)
  the two profiles are of different devices: /device:TPU:8 before, /device:TPU:2 now
where the time goes in v1:
time: 334 us; the launch traced here: 333 us
  waiting for transfers between devices  158 us (47%)
  local copies, waits for them, and re-layouts  63 us (19%)
  blocking collectives  41.2 us (12%)
  starting transfers between devices  26.5 us (8%)
  other arithmetic  15.8 us (5%)
  matrix products  14.3 us (4%)
  between operations  14.1 us (4%)
    all_gather x1, waiting for transfers between devices, sent_together(): out, at, outs = (lax.all_gather(both, axis, axis=dim, tiled=True), 0, [])  68.4 us
    all_gather x1, waiting for transfers between devices, body(): lax.all_gather(gate_up_codes, 'local')  61.3 us
    all_gather x1, blocking collectives, body(): lax.all_gather(gate_up_scales, 'local', axis=1, tiled=True)  41.2 us
    convert_element_type x2, local copies, waits for them, and re-layouts, dequant(): codes.astype(jnp.float32)  28.6 us
    all_to_all x1, waiting for transfers between devices, sent_and_summed(): lax.all_to_all(pieces, axis, split_axis=0, concat_axis=0, tiled=True)  27.6 us
    mul x2, local copies, waits for them, and re-layouts, dequant(): weight = blocked * scales.astype(jnp.float32)[..., :, None, :]  23.9 us
    convert_element_type x1, other arithmetic, dequant(): return weight.reshape(shape).astype(jnp.bfloat16)  13.3 us
    all_to_all x1, starting transfers between devices, from_everyone(): lax.all_to_all(jnp.broadcast_to(array[None], (length, *array.shape)), axi...  11.9 us
  transfers between devices with their start and end apart: 5, of which 3 were waited for; matrix products, arithmetic and copies ran while one was open for 25% of the time, Pallas kernels for 0%

profile of v1, /device:TPU:2, one launch (start us, length us, event | category | flops | bytes accessed | tf_op | source)
XLA Modules:
  0.0 332.9 jit_solution(1886687241716291709)
XLA Ops:
  7.2 0.0 copy-start.1
  7.2 0.0 all-gather.6.cloned.1.call-start
  7.2 0.7 all-gather.6.cloned.1.call-update
  7.9 0.9 copy.27
  8.8 1.3 broadcast_in_dim.2
  10.0 11.9 %all-to-all-start = ((bf16[32,128,128]{1,2,0:T(8,128)(2,1)}), bf16[32,128,128]{1,2,0:T(8,128)(2,1)S(1)}, u32[]{:S(2)}, u32[]{:S(2)}) async-start(bf16[32,128,128]{1,2,0:T(8,128)(2,1)} %broadcast_in_dim.2), calls=%async_computation | async-start | bytes 2097152 | tf_op jit(solution)/shard_map/all_to_all | solution.py:12
  22.0 0.0 all-gather.4.cloned.1.call-start
  22.0 0.0 copy-done.1
  22.0 41.2 %all_gather.14 = bf16[2,32,448]{2,0,1:T(2,128)(2,1)S(1)} all-gather(bf16[2,2,448]{2,0,1:T(2,128)(2,1)S(1)} %copy.24), channel_id=1, replica_groups=mesh['node'=32,'local'=16] {'local'}, dimensions={1}, use_global_device_ids=true | all-gather | bytes 60928 | tf_op jit(solution)/shard_map/all_gather | solution.py:62
  63.3 0.2 copy.26
  63.5 7.8 %mul.45 = f32[2,32,128,448]{2,1,3,0:T(8,128)} broadcast(f32[2,32,448]{1,2,0:T(8,128)S(1)} %copy.26), dimensions={0,1,3} | broadcast | bytes 14794752 | tf_op jit(solution)/shard_map/mul | solution.py:51
  71.3 16.1 %mul.46 = f32[2,4096,448]{1,2,0:T(8,128)} reshape(f32[2,32,128,448]{2,1,3,0:T(8,128)} %mul.45) | data formatting | bytes 29360128 | tf_op jit(solution)/shard_map/mul | solution.py:51
  87.4 61.3 %all-gather.6.cloned.1.call-done = bf16[32,256,448]{1,2,0:T(8,128)(2,1)} async-done(((bf16[2,256,448]{1,2,0:T(8,128)(2,1)}), bf16[32,256,448]{1,2,0:T(8,128)(2,1)}) %all-gather.6.cloned.1.call-update) | async-done | bytes 7340048 | tf_op jit(solution)/shard_map/all_gather | solution.py:61
  148.7 12.6 %copy.40 = f32[16,2,256,448]{2,0,3,1:T(8,128)} copy(bf16[16,2,256,448]{2,3,1,0:T(8,128)(2,1)} %bitcast.64) | data formatting | bytes 22020096 | tf_op jit(solution)/shard_map/convert_element_type | solution.py:50
  161.2 16.0 %reshape.43 = f32[2,4096,448]{1,2,0:T(8,128)} reshape(f32[2,16,256,448]{2,1,3,0:T(8,128)} %bitcast.63) | data formatting | bytes 29360128 | tf_op jit(solution)/shard_map/convert_element_type | solution.py:50
  177.2 0.0 copy-start.2
  177.2 13.3 %multiply_convert_fusion = bf16[2,4096,448]{1,2,0:T(8,128)(2,1)} fusion(f32[2,4096,448]{1,2,0:T(8,128)} %reshape.43, f32[2,4096,448]{1,2,0:T(8,128)} %mul.46), kind=kLoop, calls=%fused_computation.2 | loop fusion | flops 7340032 | bytes 36700160 | tf_op jit(solution)/shard_map/convert_element_type | solution.py:52
  190.5 0.0 all-to-all-done
  190.5 0.0 copy-start
  190.5 3.3 fusion.8
  193.8 0.0 copy-done.2
  193.8 0.9 copy-done
  194.7 1.8 fusion.12
  196.5 0.7 pad_maximum_fusion
  197.2 0.0 all-gather.4.cloned.1.call-update
  197.2 2.8 fusion.4
  200.0 2.8 fusion
  202.8 1.3 bitcast_bitcast_fusion
  204.1 9.0 %all-to-all-start.1 = ((bf16[32,128,128]{2,1,0:T(8,128)(2,1)}), bf16[32,128,128]{2,1,0:T(8,128)(2,1)S(1)}, u32[]{:S(2)}, u32[]{:S(2)}) async-start(bf16[32,128,128]{2,1,0:T(8,128)(2,1)} %bitcast_bitcast_fusion), calls=%async_computation.1 | async-start | bytes 2097152 | tf_op jit(solution)/shard_map/all_to_all | solution.py:35
  213.1 1.3 copy.31
  214.4 27.6 %all-to-all-done.1 = bf16[32,128,128]{2,1,0:T(8,128)(2,1)S(1)} async-done(((bf16[32,128,128]{2,1,0:T(8,128)(2,1)}), bf16[32,128,128]{2,1,0:T(8,128)(2,1)S(1)}, u32[]{:S(2)}, u32[]{:S(2)}) %all-to-all-start.1) | async-done | bytes 1048608 | tf_op jit(solution)/shard_map/all_to_all | solution.py:35
  242.0 5.5 %all-to-all-start.2 = ((bf16[128,16,256]{2,0,1:T(8,128)(2,1)}), bf16[128,16,256]{2,0,1:T(8,128)(2,1)S(1)}, u32[]{:S(2)}, u32[]{:S(2)}) async-start(bf16[128,16,256]{2,0,1:T(8,128)(2,1)} %copy.31), calls=%async_computation.2 | async-start | bytes 2097152 | tf_op jit(solution)/shard_map/all_to_all | solution.py:86
  247.5 0.8 reduce_sum.21
  248.3 68.4 %all-gather.4.cloned.1.call-done = bf16[2048,896]{0,1:T(8,128)(2,1)} async-done(((bf16[128,896]{0,1:T(8,128)(2,1)}), bf16[2048,896]{0,1:T(8,128)(2,1)}) %all-gather.4.cloned.1.call-update) | async-done | bytes 3670032 | tf_op jit(solution)/shard_map/all_gather | solution.py:41
  316.7 2.5 slice_bitcast_fusion.7
  319.2 2.2 copy_bitcast_fusion.1
  321.5 0.0 all-to-all-done.2
  321.5 3.6 %convert_reduce_fusion = f32[896,256]{1,0:T(8,128)S(1)} fusion(bf16[16,128,448]{1,2,0:T(8,128)(2,1)S(1)} %get-tuple-element.8, bf16[16,128,448]{1,2,0:T(8,128)(2,1)} %get-tuple-element.9, bf16[128,16,256]{2,0,1:T(8,128)(2,1)S(1)} %all-to-all-done.2), kind=kOutput, calls=%fused_computation.1 | convolution fusion | flops 957644800 | bytes 5636096 | tf_op jit(solution)/shard_map/dot_general | solution.py:94
  325.1 1.0 broadcast_multiply_fusion
  (2 shorter events, 0.0 us)
Async XLA Ops:
  7.2 14.9 %copy-start.1 = (bf16[2,2,448]{2,1,0:T(2,128)(2,1)S(1)}, bf16[2,2,448]{2,1,0:T(2,128)(2,1)}, u32[]{:S(2)}) copy-start(bf16[2,2,448]{2,1,0:T(2,128)(2,1)} %param.6) | copy-start | bytes 10756
  7.2 141.5 %all-gather.6.cloned.1.call-start = ((), (), s32[]{:S(2)}) async-start(), calls=%async_computation.4 | async-start | bytes 7798784 | tf_op jit(solution)/shard_map/all_gather | solution.py:61
  10.0 180.5 %all-to-all-start = ((bf16[32,128,128]{1,2,0:T(8,128)(2,1)}), bf16[32,128,128]{1,2,0:T(8,128)(2,1)S(1)}, u32[]{:S(2)}, u32[]{:S(2)}) async-start(bf16[32,128,128]{1,2,0:T(8,128)(2,1)} %broadcast_in_dim.2), calls=%async_computation | async-start | bytes 2097152 | tf_op jit(solution)/shard_map/all_to_all | solution.py:12
  22.0 294.7 %all-gather.4.cloned.1.call-start = ((), (), s32[]{:S(2)}) async-start(), calls=%async_computation.3 | async-start | bytes 3899392 | tf_op jit(solution)/shard_map/all_gather | solution.py:41
  177.2 16.6 %copy-start.2 = (bf16[128,448]{0,1:T(8,128)(2,1)S(1)}, bf16[128,448]{0,1:T(8,128)(2,1)}, u32[]{:S(2)}) copy-start(bf16[128,448]{0,1:T(8,128)(2,1)} %param.7) | copy-start | bytes 344068
  190.5 4.2 %copy-start = (bf16[2,4096,448]{1,2,0:T(8,128)(2,1)S(1)}, bf16[2,4096,448]{1,2,0:T(8,128)(2,1)}, u32[]{:S(2)}) copy-start(bf16[2,4096,448]{1,2,0:T(8,128)(2,1)} %multiply_convert_fusion) | copy-start | bytes 22020100
  204.1 37.9 %all-to-all-start.1 = ((bf16[32,128,128]{2,1,0:T(8,128)(2,1)}), bf16[32,128,128]{2,1,0:T(8,128)(2,1)S(1)}, u32[]{:S(2)}, u32[]{:S(2)}) async-start(bf16[32,128,128]{2,1,0:T(8,128)(2,1)} %bitcast_bitcast_fusion), calls=%async_computation.1 | async-start | bytes 2097152 | tf_op jit(solution)/shard_map/all_to_all | solution.py:35
  242.0 79.5 %all-to-all-start.2 = ((bf16[128,16,256]{2,0,1:T(8,128)(2,1)}), bf16[128,16,256]{2,0,1:T(8,128)(2,1)S(1)}, u32[]{:S(2)}, u32[]{:S(2)}) async-start(bf16[128,16,256]{2,0,1:T(8,128)(2,1)} %copy.31), calls=%async_computation.2 | async-start | bytes 2097152 | tf_op jit(solution)/shard_map/all_to_all | solution.py:86
Sparse Core Ops, SparseCore 0:
  11.2 137.4 all-gather.5
  197.3 119.3 all-gather.3
